TPU v7x, 32 devices: a whole 2x2x4 slice. The times are simulated.
32 devices in a mesh: dp: 4 (over x, core), ctx: 4 (over z), tensor: 2 (over y).
Axes of the slice: x: 2, y: 2, z: 4, core: 2. Of those that a mesh axis runs over, the one named last changes fastest.
Arguments:
- inputs: bfloat16 [8192, 768], P(('dp', 'ctx')), may hold values from -6 to 6
- segments: int32 [4, 2048], P('dp', 'ctx'), may hold values from 0 to 7, never falling along the last dimension, each value on 1 to 1536 neighbouring positions
- query_proj: bfloat16 [768, 768], P(None, 'tensor'), may hold values from -0.4375 to 0.4375
- key_proj: bfloat16 [768, 768], P(None, 'tensor'), may hold values from -0.21875 to 0.21875
- value_proj: bfloat16 [768, 768], P(None, 'tensor'), may hold values from -0.21875 to 0.21875
- query_bias: bfloat16 [768], P('tensor'), may hold values from -3 to 3
- value_bias: bfloat16 [768], P('tensor'), may hold values from -0.59765625 to 0.59765625
- output_proj: bfloat16 [768, 768], P('tensor'), may hold values from -0.875 to 0.875
- output_bias: bfloat16 [768], replicated, may hold values from -1.1953125 to 1.1953125
- attn_gain: bfloat16 [768], replicated, may hold values from 0.5 to 1.5
- attn_shift: bfloat16 [768], replicated, may hold values from -1.1953125 to 1.1953125
- expand_proj: bfloat16 [768, 3072], P(None, 'tensor'), may hold values from -0.21875 to 0.21875
- expand_bias: bfloat16 [3072], P('tensor'), may hold values from -3 to 3
- shrink_proj: bfloat16 [3072, 768], P('tensor'), may hold values from -0.109375 to 0.109375
- shrink_bias: bfloat16 [768], replicated, may hold values from -1.1953125 to 1.1953125
- final_gain: bfloat16 [768], replicated, may hold values from 0.5 to 1.5
- final_shift: bfloat16 [768], replicated, may hold values from -1.1953125 to 1.1953125
- cotangent: bfloat16 [8192, 768], P(('dp', 'ctx')), may hold values from -6 to 6
Outputs:
- output: bfloat16 [8192, 768], P(('dp', 'ctx'))
- input_grad: float32 [8192, 768], P(('dp', 'ctx'))
- query_grad: float32 [768, 768], P(None, 'tensor')
- key_grad: float32 [768, 768], P(None, 'tensor')
- value_grad: float32 [768, 768], P(None, 'tensor')
- qbias_grad: float32 [768], P('tensor')
- vbias_grad: float32 [768], P('tensor')
- oproj_grad: float32 [768, 768], P('tensor')
- obias_grad: float32 [768], replicated
- again_grad: float32 [768], replicated
- ashift_grad: float32 [768], replicated
- expand_grad: float32 [768, 3072], P(None, 'tensor')
- ebias_grad: float32 [3072], P('tensor')
- shrink_grad: float32 [3072, 768], P('tensor')
- sbias_grad: float32 [768], replicated
- fgain_grad: float32 [768], replicated
- fshift_grad: float32 [768], replicated
Inputs may be any that keep to these rules, and one draw needn't show every extreme that they name: `segments`: along each sequence the ids never fall; every id from 0 to 7 names one document of the sequence, and one document has 1536 tokens.
All inputs are finite; a program needn't handle non-finite values.
Results may differ from a plain program's by a relative error of at most 0.019.
Values may be sent and summed in bfloat16 or wider, within the bound.
A program may use at most 256 MiB of HBM per device.

v0:
```python
import jax
import jax.numpy as jnp
from jax import lax
from jax.sharding import PartitionSpec as P

HEAD_DIM = 64
norm_eps = 1e-12
masked = -1e30
contract_rows = (((0,), (0,)), ((), ()))
contract_cols = (((1,), (1,)), ((), ()))


def matmul(left, right):
    return jnp.dot(left, right, preferred_element_type=jnp.float32)


def inner_rows(left, right):
    return lax.dot_general(left, right, contract_rows, preferred_element_type=jnp.float32)


def inner_cols(left, right):
    return lax.dot_general(left, right, contract_cols, preferred_element_type=jnp.float32)


def norm_forward(values, gain, shift):
    centred = values - jnp.mean(values, axis=-1, keepdims=True)
    spread = jnp.mean(centred * centred, axis=-1, keepdims=True)
    recip = lax.rsqrt(spread + norm_eps)
    normed = centred * recip
    return (normed * gain + shift, normed, recip)


def norm_backward(upstream, normed, recip, gain):
    scaled = upstream * gain
    centred = (
        scaled
        - jnp.mean(scaled, axis=-1, keepdims=True)
        - normed * jnp.mean(scaled * normed, axis=-1, keepdims=True)
    )
    return (centred * recip, jnp.sum(upstream * normed, axis=0), jnp.sum(upstream, axis=0))


def cross_scores(left, right):
    return inner_cols(left, right)


def spread_apply(weights_in, right):
    return matmul(weights_in, right)


def spread_transpose(weights_in, left):
    return inner_rows(weights_in, left)


def body(
    inputs,
    segments,
    query_proj,
    key_proj,
    value_proj,
    query_bias,
    value_bias,
    output_proj,
    output_bias,
    attn_gain,
    attn_shift,
    expand_proj,
    expand_bias,
    shrink_proj,
    shrink_bias,
    final_gain,
    final_shift,
    cotangent,
):
    head_count = query_proj.shape[1] // HEAD_DIM
    scale = HEAD_DIM ** (-0.5)
    seg_local = segments[0]
    queries = (matmul(inputs, query_proj) + query_bias.astype(jnp.float32)).astype(jnp.bfloat16)
    keys = matmul(inputs, key_proj).astype(jnp.bfloat16)
    values = (matmul(inputs, value_proj) + value_bias.astype(jnp.float32)).astype(jnp.bfloat16)
    all_keys, all_values, key_ids = (
        lax.all_gather(keys, "ctx", axis=0, tiled=True),
        lax.all_gather(values, "ctx", axis=0, tiled=True),
        lax.all_gather(seg_local.astype(jnp.bfloat16), "ctx", axis=0, tiled=True),
    )
    query_segs = seg_local.astype(jnp.float32)
    key_segs = key_ids.astype(jnp.float32)
    same_seg = query_segs[:, None] == key_segs[None, :]

    def split_heads(matrix):
        return jnp.swapaxes(matrix.reshape(matrix.shape[0], head_count, HEAD_DIM), 0, 1)

    def join_heads(stack):
        return jnp.swapaxes(stack, 0, 1).reshape(stack.shape[1], head_count * HEAD_DIM)

    query_heads = split_heads(queries)
    key_heads = split_heads(all_keys)
    value_heads = split_heads(all_values)

    def head_forward(state, triple):
        query_head, key_head, value_head = triple
        scores = cross_scores(query_head, key_head) * scale
        scores = jnp.where(same_seg, scores, masked)
        row_max = jnp.max(scores, axis=1, keepdims=True)
        exp_scores = jnp.where(same_seg, jnp.exp(scores - row_max), 0.0)
        row_sum = jnp.sum(exp_scores, axis=1, keepdims=True)
        attn_probs = (exp_scores / row_sum).astype(jnp.bfloat16)
        mixed = spread_apply(attn_probs, value_head)
        return (state, (mixed, row_max + jnp.log(row_sum)))

    mixed_heads, log_sums = lax.scan(head_forward, None, (query_heads, key_heads, value_heads))[1]
    attended = join_heads(mixed_heads).astype(jnp.bfloat16)
    attn_total = lax.psum(matmul(attended, output_proj).astype(jnp.bfloat16), "tensor").astype(
        jnp.float32
    )
    attn_gain_f = attn_gain.astype(jnp.float32)
    first, first_normed, first_recip = norm_forward(
        inputs.astype(jnp.float32) + attn_total + output_bias.astype(jnp.float32),
        attn_gain_f,
        attn_shift.astype(jnp.float32),
    )
    first_low = first.astype(jnp.bfloat16)
    pre_act = matmul(first_low, expand_proj) + expand_bias.astype(jnp.float32)
    activated, gelu_back = jax.vjp(lambda pre_in: jax.nn.gelu(pre_in, approximate=False), pre_act)
    hidden = activated.astype(jnp.bfloat16)
    feed_total = lax.psum(matmul(hidden, shrink_proj).astype(jnp.bfloat16), "tensor").astype(
        jnp.float32
    )
    second = first + feed_total + shrink_bias.astype(jnp.float32)
    final_gain_f = final_gain.astype(jnp.float32)
    output, second_normed, second_recip = norm_forward(
        second, final_gain_f, final_shift.astype(jnp.float32)
    )
    upstream = cotangent.astype(jnp.float32)
    grad_second, fgain_grad, fshift_grad = norm_backward(
        upstream, second_normed, second_recip, final_gain_f
    )
    sbias_grad = jnp.sum(grad_second, axis=0)
    grad_second_low = grad_second.astype(jnp.bfloat16)
    shrink_grad = inner_rows(hidden, grad_second_low)
    grad_act = inner_cols(grad_second_low, shrink_proj)
    grad_pre = gelu_back(grad_act)[0].astype(jnp.bfloat16)
    ebias_grad = jnp.sum(grad_pre.astype(jnp.float32), axis=0)
    expand_grad = inner_rows(first_low, grad_pre)
    grad_first = grad_second + lax.psum(
        inner_cols(grad_pre, expand_proj).astype(jnp.bfloat16), "tensor"
    ).astype(jnp.float32)
    grad_mix, again_grad, ashift_grad = norm_backward(
        grad_first, first_normed, first_recip, attn_gain_f
    )
    obias_grad = jnp.sum(grad_mix, axis=0)
    grad_mix_low = grad_mix.astype(jnp.bfloat16)
    oproj_grad = inner_rows(attended, grad_mix_low)
    grad_attended = inner_cols(grad_mix_low, output_proj).astype(jnp.bfloat16)
    grad_heads = split_heads(grad_attended)

    def head_backward(state, group):
        query_head, key_head, value_head, grad_head, log_sum = group
        scores = cross_scores(query_head, key_head) * scale
        attn_probs = jnp.where(same_seg, jnp.exp(scores - log_sum), 0.0)
        grad_probs = cross_scores(grad_head, value_head)
        row_dot = jnp.sum(attn_probs * grad_probs, axis=1, keepdims=True)
        grad_scores = (attn_probs * (grad_probs - row_dot)).astype(jnp.bfloat16)
        grad_query = spread_apply(grad_scores, key_head) * scale
        grad_key = spread_transpose(grad_scores, query_head) * scale
        grad_value = spread_transpose(attn_probs.astype(jnp.bfloat16), grad_head)
        return (state, (grad_query, grad_key, grad_value))

    query_back, key_back, value_back = lax.scan(
        head_backward, None, (query_heads, key_heads, value_heads, grad_heads, log_sums)
    )[1]
    grad_queries = join_heads(query_back).astype(jnp.bfloat16)
    key_sum, value_sum = (
        lax.psum_scatter(
            join_heads(key_back).astype(jnp.bfloat16), "ctx", scatter_dimension=0, tiled=True
        ).astype(jnp.float32),
        lax.psum_scatter(
            join_heads(value_back).astype(jnp.bfloat16), "ctx", scatter_dimension=0, tiled=True
        ).astype(jnp.float32),
    )
    grad_keys = key_sum.astype(jnp.bfloat16)
    grad_values = value_sum.astype(jnp.bfloat16)
    qbias_grad = jnp.sum(grad_queries.astype(jnp.float32), axis=0)
    vbias_grad = jnp.sum(grad_values.astype(jnp.float32), axis=0)
    query_grad = inner_rows(inputs, grad_queries)
    key_grad = inner_rows(inputs, grad_keys)
    value_grad = inner_rows(inputs, grad_values)
    back_terms = (
        inner_cols(grad_queries, query_proj)
        + inner_cols(grad_keys, key_proj)
        + inner_cols(grad_values, value_proj)
    )
    input_grad = grad_mix + lax.psum(back_terms.astype(jnp.bfloat16), "tensor").astype(jnp.float32)
    (
        query_grad,
        key_grad,
        value_grad,
        qbias_grad,
        vbias_grad,
        oproj_grad,
        obias_grad,
        again_grad,
        ashift_grad,
        expand_grad,
        ebias_grad,
        shrink_grad,
        sbias_grad,
        fgain_grad,
        fshift_grad,
    ) = lax.psum(
        (
            query_grad,
            key_grad,
            value_grad,
            qbias_grad,
            vbias_grad,
            oproj_grad,
            obias_grad,
            again_grad,
            ashift_grad,
            expand_grad,
            ebias_grad,
            shrink_grad,
            sbias_grad,
            fgain_grad,
            fshift_grad,
        ),
        ("dp", "ctx"),
    )
    return (
        output.astype(jnp.bfloat16),
        input_grad,
        query_grad,
        key_grad,
        value_grad,
        qbias_grad,
        vbias_grad,
        oproj_grad,
        obias_grad,
        again_grad,
        ashift_grad,
        expand_grad,
        ebias_grad,
        shrink_grad,
        sbias_grad,
        fgain_grad,
        fshift_grad,
    )


def solution(mesh):
    in_specs = (
        P(("dp", "ctx"), None),
        P("dp", "ctx"),
        P(None, "tensor"),
        P(None, "tensor"),
        P(None, "tensor"),
        P("tensor"),
        P("tensor"),
        P("tensor", None),
        P(),
        P(),
        P(),
        P(None, "tensor"),
        P("tensor"),
        P("tensor", None),
        P(),
        P(),
        P(),
        P(("dp", "ctx"), None),
    )
    out_specs = (
        P(("dp", "ctx"), None),
        P(("dp", "ctx"), None),
        P(None, "tensor"),
        P(None, "tensor"),
        P(None, "tensor"),
        P("tensor"),
        P("tensor"),
        P("tensor", None),
        P(),
        P(),
        P(),
        P(None, "tensor"),
        P("tensor"),
        P("tensor", None),
        P(),
        P(),
        P(),
    )
    return jax.shard_map(body, mesh=mesh, in_specs=in_specs, out_specs=out_specs, check_vma=False)
```

profile of v0, /device:TPU:0, one launch (start us, length us, event | category | flops | bytes accessed | tf_op | source)
XLA Modules:
  0.0 743.4 jit_solution(2113761524882374570)
XLA Ops:
  7.3 2.8 convolution_convert_fusion.4
  12.7 13.7 %all-gather = bf16[1,2048]{1,0:T(2,128)(2,1)S(1)} all-gather(bf16[1,512]{1,0:T(2,128)(2,1)S(1)} %get-tuple-element.288), channel_id=2, replica_groups=mesh['dp'=4,'ctx'=4,'tensor'=2] {'ctx'}, dimensions={1}, use_global_device_ids=true | all-gather | bytes 5120 | tf_op jit(solution)/shard_map/all_gather | solution.py:84
  29.1 21.0 %all-gather.4.cloned.1.call-done = bf16[2048,384]{1,0:T(8,128)(2,1)} async-done(((bf16[512,384]{1,0:T(8,128)(2,1)}), bf16[2048,384]{1,0:T(8,128)(2,1)}) %all-gather.4.cloned.1.call-update) | async-done | bytes 1572880 | tf_op jit(solution)/shard_map/all_gather | solution.py:82
  52.6 4.1 copy.45
  56.8 31.5 %all-gather.6.cloned.1.call-done = bf16[2048,384]{1,0:T(8,128)(2,1)} async-done(((bf16[512,384]{1,0:T(8,128)(2,1)}), bf16[2048,384]{1,0:T(8,128)(2,1)}) %all-gather.6.cloned.1.call-update) | async-done | bytes 1572880 | tf_op jit(solution)/shard_map/all_gather | solution.py:83
  90.8 4.1 copy.46
  94.9 38.4 %while.28 = (s32[]{:T(128)}, bf16[6,512,64]{1,2,0:T(8,128)(2,1)S(1)}, f32[6,512,1]{1,2,0:T(1,128)}, bf16[6,512,64]{2,1,0:T(8,128)(2,1)}, bf16[6,2048,64]{2,1,0:T...) while((s32[]{:T(128)}, ...), condition=%wide.region_3.4_spmd.clone, body=%wide.region_0.3_spmd.clone.sunk | while | flops 286260736 | bytes 13946985 | solution.py:111
  140.6 28.8 %all-reduce.8.cloned.1.call-done = bf16[512,768]{1,0:T(8,128)(2,1)} async-done(((bf16[512,768]{1,0:T(8,128)(2,1)}), bf16[512,768]{1,0:T(8,128)(2,1)}) %all-reduce.8.cloned.1.call-update) | async-done | bytes 786448 | tf_op jit(solution)/shard_map/psum | solution.py:113
  171.5 9.5 %multiply_convert_fusion.1 = (bf16[512,1536]{1,0:T(8,128)(2,1)S(1)}, f32[512,1536]{1,0:T(8,128)}, f32[512,1536]{1,0:T(8,128)}) fusion(f32[1536]{0:T(1024)S(1)} %copy-done.41, bf16[768,1536]{1,0:T(8,128)(2,1)S(1)} %copy-done, f32[768]{0:T(1024)S(1)} %copy-done.38, f32[768]{0:T(1024)S(1)} %copy-done.23, f32[512]{0:T(512)S(1)} %add_rsqrt_fusion.1, ...), kind=kOutput, calls=%fused_computation.62 | convolution fusion | flops 1263403008 | bytes 11815936 | tf_op jit(solution)/shard_map/dot_general | solution.py:14
  184.8 34.2 %all-reduce.10.cloned.1.call-done = bf16[512,768]{1,0:T(8,128)(2,1)} async-done(((bf16[512,768]{1,0:T(8,128)(2,1)}), bf16[512,768]{1,0:T(8,128)(2,1)}) %all-reduce.10.cloned.1.call-update) | async-done | bytes 786448 | tf_op jit(solution)/shard_map/psum | solution.py:126
  225.0 2.9 convert_reduce_fusion
  231.5 34.4 %all-reduce.12.cloned.1.call-done = bf16[512,768]{1,0:T(8,128)(2,1)} async-done(((bf16[512,768]{1,0:T(8,128)(2,1)}), bf16[512,768]{1,0:T(8,128)(2,1)}) %all-reduce.12.cloned.1.call-update) | async-done | bytes 786448 | tf_op jit(solution)/shard_map/psum | solution.py:145
  265.9 3.5 multiply_reduce_fusion.1
  273.7 70.0 %while.29 = (s32[]{:T(128)}, bf16[6,512,64]{1,2,0:T(8,128)(2,1)S(1)}, bf16[6,2048,64]{1,2,0:T(8,128)(2,1)}, bf16[6,2048,64]{1,2,0:T(8,128)(2,1)}, bf16[6,512,64]...) while((s32[]{:T(128)}, ...), condition=%wide.region_17.18_spmd.clone, body=%wide.region_15.17_spmd.clone.sunk | while | flops 681737728 | bytes 34759808 | solution.py:169
  345.1 5.1 fusion.67
  350.3 3.8 fusion.73
  357.4 21.8 %reduce-scatter.3.cloned.1.call-done = bf16[512,384]{0,1:T(8,128)(2,1)} async-done(((bf16[2048,384]{0,1:T(8,128)(2,1)}), bf16[512,384]{0,1:T(8,128)(2,1)}) %reduce-scatter.3.cloned.1.call-update) | async-done | bytes 393232 | tf_op jit(solution)/shard_map/reduce_scatter | solution.py:174
  379.1 3.0 fusion.82
  382.1 33.8 %reduce-scatter.5.cloned.1.call-done = bf16[512,384]{0,1:T(8,128)(2,1)} async-done(((bf16[2048,384]{0,1:T(8,128)(2,1)}), bf16[512,384]{0,1:T(8,128)(2,1)}) %reduce-scatter.5.cloned.1.call-update) | async-done | bytes 393232 | tf_op jit(solution)/shard_map/reduce_scatter | solution.py:177
  415.8 3.5 add_convert_fusion.1
  424.7 61.2 %all-reduce = (f32[384]{0:T(512)}, f32[384]{0:T(512)}, f32[768]{0:T(1024)}, f32[768]{0:T(1024)}, f32[768]{0:T(1024)}, /*index=5*/f32[1536]{0:T(1024)}, f32[768]{0:T(1024)}, f32[768]{0:T(1024)}, f32[768]{0:T(1024)}) all-reduce(f32[384]{0:T(512)S(1)} %reduce_sum.182, ...), channel_id=1, replica_groups=mesh['dp'=4,'ctx'=4,'tensor'=2] {'dp','ctx'}, use_global_device_ids=true, to_apply=%region_25.26 | all-reduce | flops 6912 | bytes 55296 | tf_op jit(solution)/shard_map/psum | solution.py:210
  488.3 231.7 %all-reduce.16.cloned.1.call-done = (f32[768,384]{0,1:T(8,128)}, f32[768,384]{0,1:T(8,128)}, f32[768,384]{0,1:T(8,128)}, f32[384,768]{1,0:T(8,128)}, f32[768,1536]{1,0:T(8,128)}, /*index=5*/f32[1536,768]{1,0:T(8,128)}) async-done(((f32[768,384]{0,1:T(8,128)}, f32[768,384]{0,1:T(8,128)}, f32[768,384]{0,1:T(8,128)}, f32[384,768]{1,0:T(8,128)}, f32[768,1536]{1,0:T(8,128)}, /*index=5*/f32[1536,768]{1,0:T(8,128)}), ...) | async-done | bytes 14155792 | tf_op jit(solution)/shard_map/psum | solution.py:210
  720.1 2.7 copy.50
  728.0 5.5 copy.92
  (259 shorter events, 166.2 us)
Async XLA Ops:
  7.2 164.2 %copy-start = (bf16[768,1536]{1,0:T(8,128)(2,1)S(1)}, bf16[768,1536]{1,0:T(8,128)(2,1)}, u32[]{:S(2)}) copy-start(bf16[768,1536]{1,0:T(8,128)(2,1)} %param.33) | copy-start | bytes 7077892
  7.2 42.8 %all-gather.4.cloned.1.call-start = ((), (), s32[]{:S(2)}) async-start(), calls=%async_computation.2 | async-start | bytes 1966080 | tf_op jit(solution)/shard_map/all_gather | solution.py:82
  10.1 78.1 %all-gather.6.cloned.1.call-start = ((), (), s32[]{:S(2)}) async-start(), calls=%async_computation.3 | async-start | bytes 1966080 | tf_op jit(solution)/shard_map/all_gather | solution.py:83
  12.6 156.8 %all-reduce.8.cloned.1.call-start = ((), (), s32[]{:S(2)}) async-start(), calls=%async_computation.4 | async-start | bytes 1572864 | tf_op jit(solution)/shard_map/psum | solution.py:113
  133.3 38.1 %copy-start.12 = (bf16[6,512,64]{1,2,0:T(8,128)(2,1)}, bf16[6,512,64]{1,2,0:T(8,128)(2,1)S(1)}, u32[]{:S(2)}) copy-start(bf16[6,512,64]{1,2,0:T(8,128)(2,1)S(1)} %get-tuple-element.109) | copy-start | bytes 1179652
  136.0 83.0 %all-reduce.10.cloned.1.call-start = ((), (), s32[]{:S(2)}) async-start(), calls=%async_computation.5 | async-start | bytes 1572864 | tf_op jit(solution)/shard_map/psum | solution.py:126
  170.9 10.1 %copy-start.26 = (f32[512]{0:T(512)}, f32[512]{0:T(512)S(1)}, u32[]{:S(2)}) copy-start(f32[512]{0:T(512)S(1)} %broadcast_multiply_fusion.5) | copy-start | bytes 6148
  171.5 9.6 %copy-start.29 = (f32[512]{0:T(512)}, f32[512]{0:T(512)S(1)}, u32[]{:S(2)}) copy-start(f32[512]{0:T(512)S(1)} %add_rsqrt_fusion.1) | copy-start | bytes 6148
  171.5 10.7 %copy-start.49 = (bf16[1536,768]{1,0:T(8,128)(2,1)S(1)}, bf16[1536,768]{1,0:T(8,128)(2,1)}, u32[]{:S(2)}) copy-start(bf16[1536,768]{1,0:T(8,128)(2,1)} %param.35) | copy-start | bytes 7077892
  182.2 36.8 %copy-start.24 = (f32[768]{0:T(1024)S(1)}, f32[768]{0:T(1024)}, u32[]{:S(2)}) copy-start(f32[768]{0:T(1024)} %convert_element_type.185) | copy-start | bytes 9220
  182.2 36.8 %copy-start.27 = (f32[512]{0:T(512)S(1)}, f32[512]{0:T(512)}, u32[]{:S(2)}) copy-start(f32[512]{0:T(512)} %copy-done.26) | copy-start | bytes 6148
  182.2 36.8 %copy-start.30 = (f32[512]{0:T(512)S(1)}, f32[512]{0:T(512)}, u32[]{:S(2)}) copy-start(f32[512]{0:T(512)} %copy-done.29) | copy-start | bytes 6148
  182.2 36.8 %copy-start.39 = (f32[768]{0:T(1024)S(1)}, f32[768]{0:T(1024)}, u32[]{:S(2)}) copy-start(f32[768]{0:T(1024)} %convert_element_type.186) | copy-start | bytes 9220
  184.5 81.4 %all-reduce.12.cloned.1.call-start = ((), (), s32[]{:S(2)}) async-start(), calls=%async_computation.6 | async-start | bytes 1572864 | tf_op jit(solution)/shard_map/psum | solution.py:145
  231.4 38.0 %copy-start.4 = (f32[512,768]{1,0:T(8,128)S(1)}, f32[512,768]{1,0:T(8,128)}, u32[]{:S(2)}) copy-start(f32[512,768]{1,0:T(8,128)} %copy-done.3) | copy-start | bytes 4718596
  231.4 38.0 %copy-start.9 = (bf16[512,768]{1,0:T(8,128)(2,1)S(1)}, bf16[512,768]{1,0:T(8,128)(2,1)}, u32[]{:S(2)}) copy-start(bf16[512,768]{1,0:T(8,128)(2,1)} %all-reduce.8.cloned.1.call-done) | copy-start | bytes 2359300
  231.4 147.7 %reduce-scatter.3.cloned.1.call-start = ((), (), s32[]{:S(2)}) async-start(), calls=%async_computation.7 | async-start | bytes 1966080 | tf_op jit(solution)/shard_map/reduce_scatter | solution.py:174
  343.7 72.2 %reduce-scatter.5.cloned.1.call-start = ((), (), s32[]{:S(2)}) async-start(), calls=%async_computation.8 | async-start | bytes 1966080 | tf_op jit(solution)/shard_map/reduce_scatter | solution.py:177
  344.4 5.8 copy-start.10
  344.4 5.8 copy-start.25
  344.5 141.4 %all-reduce.14.cloned.1.call-start = ((), (), s32[]{:S(2)}) async-start(), calls=%async_computation.9 | async-start | bytes 1572864 | tf_op jit(solution)/shard_map/psum | solution.py:193
  357.4 58.5 %copy-start.21 = (bf16[768,384]{1,0:T(8,128)(2,1)S(1)}, bf16[768,384]{1,0:T(8,128)(2,1)}, u32[]{:S(2)}) copy-start(bf16[768,384]{1,0:T(8,128)(2,1)} %param.26) | copy-start | bytes 1769476
  419.4 300.7 %all-reduce.16.cloned.1.call-start = ((), (), s32[]{:S(2)}) async-start(), calls=%async_computation.10 | async-start | bytes 28311552 | tf_op jit(solution)/shard_map/psum | solution.py:210
  727.0 6.5 slice-start
  (42 other events, 115.0 us)
Sparse Core Ops, SparseCore 0:
  10.2 39.8 all-gather.3
  52.2 35.9 all-gather.5
  136.1 33.1 all-reduce.7
  184.7 34.3 all-reduce.9
  231.5 34.3 all-reduce.11
  343.8 35.2 reduce-scatter.2
  381.5 34.2 reduce-scatter.4
  419.5 33.2 all-reduce.13
  459.1 260.8 all-reduce.15
where the time goes:
time: 746 us; the launch traced here: 743 us
  waiting for transfers between devices  438 us (59%)
  matrix products  141 us (19%)
  blocking collectives  74.9 us (10%)
  local copies, waits for them, and re-layouts  44.8 us (6%)
  other arithmetic  29.9 us (4%)
  between operations  14.4 us (2%)
    psum x1, waiting for transfers between devices, body(): lax.psum((query_grad, key_grad, value_grad, qbias_grad, vbias_grad, oproj...  232 us
    psum x1, blocking collectives, body(): lax.psum((query_grad, key_grad, value_grad, qbias_grad, vbias_grad, oproj...  61.2 us
    dot_general x24, matrix products, inner_cols(): lax.dot_general(left, right, contract_cols, preferred_element_type=jnp.fl...  52.3 us
    dot_general x18, matrix products, matmul(): return jnp.dot(left, right, preferred_element_type=jnp.float32)  47.6 us
    dot_general x18, matrix products, inner_rows(): lax.dot_general(left, right, contract_rows, preferred_element_type=jnp.fl...  40.7 us
    psum x1, waiting for transfers between devices, body(): lax.psum(inner_cols(grad_pre, expand_proj).astype(jnp.bfloat16), 'tensor')  34.4 us
    psum x1, waiting for transfers between devices, body(): lax.psum(matmul(hidden, shrink_proj).astype(jnp.bfloat16), 'tensor')  34.2 us
    reduce_scatter x1, waiting for transfers between devices, body(): lax.psum_scatter(join_heads(value_back).astype(jnp.bfloat16), 'ctx', scat...  33.8 us
  transfers between devices with their start and end apart: 9, of which 8 were waited for; matrix products, arithmetic and copies ran while one was open for 5% of the time, Pallas kernels for 0%

commit v1 on v0

--- a/solution.py
+++ b/solution.py
@@ -8,6 +8,28 @@
 masked = -1e30
 contract_rows = (((0,), (0,)), ((), ()))
 contract_cols = (((1,), (1,)), ((), ()))
+
+
+def in_order(blocks, dim):
+    lengths = list(blocks.shape[1:])
+    lengths[dim] *= blocks.shape[0]
+    return jnp.moveaxis(blocks, 0, dim).reshape(lengths)
+
+
+def ring_gather(shard, axis, dim):
+    size = lax.axis_size(axis)
+    pairs = [(i, (i + 1) % size) for i in range(size)]
+    back = [(b, a) for a, b in pairs]
+    lower, upper = ([], [])
+    for lap in range(size - 1):
+        if lap % 2 == 0:
+            lower.append(lax.ppermute(lower[-1] if lower else shard, axis, pairs))
+        else:
+            upper.append(lax.ppermute(upper[-1] if upper else shard, axis, back))
+    parts = jnp.stack([*lower[::-1], shard, *upper])
+    shift = lax.axis_index(axis) - len(lower)
+    parts = parts[(jnp.arange(size) - shift) % size]
+    return in_order(parts, dim)
 
 
 def matmul(left, right):
@@ -79,7 +101,7 @@
     keys = matmul(inputs, key_proj).astype(jnp.bfloat16)
     values = (matmul(inputs, value_proj) + value_bias.astype(jnp.float32)).astype(jnp.bfloat16)
     all_keys, all_values, key_ids = (
-        lax.all_gather(keys, "ctx", axis=0, tiled=True),
+        ring_gather(keys, "ctx", 0),
         lax.all_gather(values, "ctx", axis=0, tiled=True),
         lax.all_gather(seg_local.astype(jnp.bfloat16), "ctx", axis=0, tiled=True),
     )

time: 746 us -> 745 us (level)
  waiting for transfers between devices: 438 us -> 392 us
  blocking collectives: 74.9 us -> 101 us
  local copies, waits for them, and re-layouts: 44.8 us -> 54.6 us
    all_gather x1, waiting for transfers between devices: 31.5 us -> 0.01 us  [body(): lax.all_gather(values, 'ctx', axis=0, tiled=True)]
    all_gather x1, blocking collectives: 13.7 us -> 39.5 us  [body(): lax.all_gather(seg_local.astype(jnp.bfloat16), 'ctx', axis=0, tiled=True)]
    all_gather x1 -> x0, waiting for transfers between devices: 21 us -> none  [body(): lax.all_gather(keys, 'ctx', axis=0, tiled=True)]
    ppermute x0 -> x3, waiting for transfers between devices: none -> 7.66 us  [the longest x2 7.66 us: ring_gather(): lower.append(lax.ppermute(lower[-1] if lower else shard, axis, pairs))]
    unnamed x122 -> x120, local copies, waits for them, and re-layouts: 29.6 us -> 30 us
  transfers between devices with their start and end apart: 9 -> 11, of which waited for: 8 -> 7; matrix products, arithmetic and copies ran while one was open for 5% -> 7% of each run, Pallas kernels for 0% -> 0%
where the time goes in v1:
time: 745 us; the launch traced here: 743 us
  waiting for transfers between devices  392 us (53%)
  matrix products  140 us (19%)
  blocking collectives  101 us (14%)
  local copies, waits for them, and re-layouts  54.6 us (7%)
  other arithmetic  33.4 us (4%)
  between operations  14.7 us (2%)
    psum x1, waiting for transfers between devices, body(): lax.psum((query_grad, key_grad, value_grad, qbias_grad, vbias_grad, oproj...  231 us
    psum x1, blocking collectives, body(): lax.psum((query_grad, key_grad, value_grad, qbias_grad, vbias_grad, oproj...  61.5 us
    dot_general x24, matrix products, inner_cols(): lax.dot_general(left, right, contract_cols, preferred_element_type=jnp.fl...  52.3 us
    dot_general x18, matrix products, matmul(): return jnp.dot(left, right, preferred_element_type=jnp.float32)  47.4 us
    dot_general x18, matrix products, inner_rows(): lax.dot_general(left, right, contract_rows, preferred_element_type=jnp.fl...  40.6 us
    all_gather x1, blocking collectives, body(): lax.all_gather(seg_local.astype(jnp.bfloat16), 'ctx', axis=0, tiled=True)  39.5 us
    psum x1, waiting for transfers between devices, body(): lax.psum(matmul(hidden, shrink_proj).astype(jnp.bfloat16), 'tensor')  34.4 us
    psum x1, waiting for transfers between devices, body(): lax.psum(inner_cols(grad_pre, expand_proj).astype(jnp.bfloat16), 'tensor')  34.1 us
  transfers between devices with their start and end apart: 11, of which 7 were waited for; matrix products, arithmetic and copies ran while one was open for 7% of the time, Pallas kernels for 0%

profile of v1, /device:TPU:0, one launch (start us, length us, event | category | flops | bytes accessed | tf_op | source)
XLA Modules:
  0.0 742.7 jit_solution(14951259654134687632)
XLA Ops:
  12.5 3.1 collective-permute-start
  17.7 39.5 %all-gather = bf16[1,2048]{1,0:T(2,128)(2,1)S(1)} all-gather(bf16[1,512]{1,0:T(2,128)(2,1)S(1)} %get-tuple-element.288), channel_id=2, replica_groups=mesh['dp'=4,'ctx'=4,'tensor'=2] {'ctx'}, dimensions={1}, use_global_device_ids=true | all-gather | bytes 5120 | tf_op jit(solution)/shard_map/all_gather | solution.py:106
  61.8 7.7 %collective-permute-done.1 = bf16[512,384]{1,0:T(8,128)(2,1)} collective-permute-done((bf16[512,384]{1,0:T(8,128)(2,1)}, bf16[512,384]{1,0:T(8,128)(2,1)}, u32[]{:S(2)}, u32[]{:S(2)}) %collective-permute-start.1) | collective-permute-done | bytes 393248 | tf_op jit(solution)/shard_map/ppermute | solution.py:26
  72.1 3.3 gather_fusion
  75.4 3.9 copy.43
  79.3 3.8 reshape_reshape.3
  83.1 4.1 copy.45
  89.7 4.1 copy.46
  93.9 38.4 %while.28 = (s32[]{:T(128)}, bf16[6,512,64]{1,2,0:T(8,128)(2,1)S(1)}, f32[6,512,1]{1,2,0:T(1,128)}, bf16[6,512,64]{2,1,0:T(8,128)(2,1)}, bf16[6,2048,64]{2,1,0:T...) while((s32[]{:T(128)}, ...), condition=%wide.region_3.4_spmd.clone, body=%wide.region_0.3_spmd.clone.sunk | while | flops 286260736 | bytes 13946985 | solution.py:133
  139.7 28.9 %all-reduce.8.cloned.1.call-done = bf16[512,768]{1,0:T(8,128)(2,1)} async-done(((bf16[512,768]{1,0:T(8,128)(2,1)}), bf16[512,768]{1,0:T(8,128)(2,1)}) %all-reduce.8.cloned.1.call-update) | async-done | bytes 786448 | tf_op jit(solution)/shard_map/psum | solution.py:135
  170.7 9.5 %multiply_convert_fusion.1 = (bf16[512,1536]{1,0:T(8,128)(2,1)S(1)}, f32[512,1536]{1,0:T(8,128)}, f32[512,1536]{1,0:T(8,128)}) fusion(f32[1536]{0:T(1024)S(1)} %copy-done.41, bf16[768,1536]{1,0:T(8,128)(2,1)S(1)} %copy-done, f32[768]{0:T(1024)S(1)} %copy-done.38, f32[768]{0:T(1024)S(1)} %copy-done.23, f32[512]{0:T(512)S(1)} %add_rsqrt_fusion.1, ...), kind=kOutput, calls=%fused_computation.63 | convolution fusion | flops 1263403008 | bytes 11815936 | tf_op jit(solution)/shard_map/dot_general | solution.py:36
  183.9 34.4 %all-reduce.10.cloned.1.call-done = bf16[512,768]{1,0:T(8,128)(2,1)} async-done(((bf16[512,768]{1,0:T(8,128)(2,1)}), bf16[512,768]{1,0:T(8,128)(2,1)}) %all-reduce.10.cloned.1.call-update) | async-done | bytes 786448 | tf_op jit(solution)/shard_map/psum | solution.py:148
  230.9 34.1 %all-reduce.12.cloned.1.call-done = bf16[512,768]{1,0:T(8,128)(2,1)} async-done(((bf16[512,768]{1,0:T(8,128)(2,1)}), bf16[512,768]{1,0:T(8,128)(2,1)}) %all-reduce.12.cloned.1.call-update) | async-done | bytes 786448 | tf_op jit(solution)/shard_map/psum | solution.py:167
  265.1 3.5 multiply_reduce_fusion.1
  272.9 69.9 %while.29 = (s32[]{:T(128)}, bf16[6,512,64]{1,2,0:T(8,128)(2,1)S(1)}, bf16[6,2048,64]{1,2,0:T(8,128)(2,1)}, bf16[6,2048,64]{1,2,0:T(8,128)(2,1)}, bf16[6,512,64]...) while((s32[]{:T(128)}, ...), condition=%wide.region_17.18_spmd.clone, body=%wide.region_15.17_spmd.clone.sunk | while | flops 681737728 | bytes 34759808 | solution.py:191
  344.2 5.1 fusion.67
  349.4 3.8 fusion.73
  356.5 21.8 %reduce-scatter.3.cloned.1.call-done = bf16[512,384]{0,1:T(8,128)(2,1)} async-done(((bf16[2048,384]{0,1:T(8,128)(2,1)}), bf16[512,384]{0,1:T(8,128)(2,1)}) %reduce-scatter.3.cloned.1.call-update) | async-done | bytes 393232 | tf_op jit(solution)/shard_map/reduce_scatter | solution.py:196
  378.3 3.0 fusion.84
  381.2 33.6 %reduce-scatter.5.cloned.1.call-done = bf16[512,384]{0,1:T(8,128)(2,1)} async-done(((bf16[2048,384]{0,1:T(8,128)(2,1)}), bf16[512,384]{0,1:T(8,128)(2,1)}) %reduce-scatter.5.cloned.1.call-update) | async-done | bytes 393232 | tf_op jit(solution)/shard_map/reduce_scatter | solution.py:199
  414.8 3.5 add_convert_fusion.1
  423.9 61.5 %all-reduce = (f32[384]{0:T(512)}, f32[384]{0:T(512)}, f32[768]{0:T(1024)}, f32[768]{0:T(1024)}, f32[768]{0:T(1024)}, /*index=5*/f32[1536]{0:T(1024)}, f32[768]{0:T(1024)}, f32[768]{0:T(1024)}, f32[768]{0:T(1024)}) all-reduce(f32[384]{0:T(512)S(1)} %reduce_sum.182, ...), channel_id=1, replica_groups=mesh['dp'=4,'ctx'=4,'tensor'=2] {'dp','ctx'}, use_global_device_ids=true, to_apply=%region_25.26 | all-reduce | flops 6912 | bytes 55296 | tf_op jit(solution)/shard_map/psum | solution.py:232
  487.9 231.2 %all-reduce.16.cloned.1.call-done = (f32[768,384]{0,1:T(8,128)}, f32[768,384]{0,1:T(8,128)}, f32[768,384]{0,1:T(8,128)}, f32[384,768]{1,0:T(8,128)}, f32[768,1536]{1,0:T(8,128)}, /*index=5*/f32[1536,768]{1,0:T(8,128)}) async-done(((f32[768,384]{0,1:T(8,128)}, f32[768,384]{0,1:T(8,128)}, f32[768,384]{0,1:T(8,128)}, f32[384,768]{1,0:T(8,128)}, f32[768,1536]{1,0:T(8,128)}, /*index=5*/f32[1536,768]{1,0:T(8,128)}), ...) | async-done | bytes 14155792 | tf_op jit(solution)/shard_map/psum | solution.py:232
  727.0 5.5 copy.92
  (265 shorter events, 178.9 us)
Async XLA Ops:
  7.2 163.5 %copy-start = (bf16[768,1536]{1,0:T(8,128)(2,1)S(1)}, bf16[768,1536]{1,0:T(8,128)(2,1)}, u32[]{:S(2)}) copy-start(bf16[768,1536]{1,0:T(8,128)(2,1)} %param.33) | copy-start | bytes 7077892
  7.2 80.0 %all-gather.3.cloned.1.call-start = ((), (), s32[]{:S(2)}) async-start(), calls=%async_computation.2 | async-start | bytes 1966080 | tf_op jit(solution)/shard_map/all_gather | solution.py:105
  8.1 9.6 %copy-start.47 = (bf16[384]{0:T(512)(128)(2,1)S(1)}, bf16[384]{0:T(512)(128)(2,1)}, u32[]{:S(2)}) copy-start(bf16[384]{0:T(512)(128)(2,1)} %param.27) | copy-start | bytes 2308
  8.1 9.6 %copy-start.43 = (s32[1,512]{1,0:T(1,128)S(1)}, s32[1,512]{1,0:T(1,128)}, u32[]{:S(2)}) copy-start(s32[1,512]{1,0:T(1,128)} %param.23) | copy-start | bytes 6148
  10.8 157.8 %all-reduce.8.cloned.1.call-start = ((), (), s32[]{:S(2)}) async-start(), calls=%async_computation.3 | async-start | bytes 1572864 | tf_op jit(solution)/shard_map/psum | solution.py:135
  12.5 44.7 %collective-permute-start = (bf16[512,384]{1,0:T(8,128)(2,1)S(1)}, bf16[512,384]{1,0:T(8,128)(2,1)}, u32[]{:S(2)}, u32[]{:S(2)}) collective-permute-start(bf16[512,384]{1,0:T(8,128)(2,1)S(1)} %convolution_convert_fusion.4), channel_id=1, source_target_pairs={{0,2},{2,4},{4,6},{6,0},{1,3},{3,5},{5,7},{7,1},{8,10},{10,12},{12... | collective-permute-start | bytes 1179656 | tf_op jit(solution)/shard_map/ppermute | solution.py:26
  15.6 46.2 %collective-permute-start.2 = (bf16[512,384]{1,0:T(8,128)(2,1)S(1)}, bf16[512,384]{1,0:T(8,128)(2,1)}, u32[]{:S(2)}, u32[]{:S(2)}) collective-permute-start(bf16[512,384]{1,0:T(8,128)(2,1)S(1)} %convolution_convert_fusion.4), channel_id=1, source_target_pairs={{2,0},{4,2},{6,4},{0,6},{3,1},{5,3},{7,5},{1,7},{10,8},{12,10},{14... | collective-permute-start | bytes 1179656 | tf_op jit(solution)/shard_map/ppermute | solution.py:28
  57.2 12.2 %collective-permute-start.1 = (bf16[512,384]{1,0:T(8,128)(2,1)}, bf16[512,384]{1,0:T(8,128)(2,1)}, u32[]{:S(2)}, u32[]{:S(2)}) collective-permute-start(bf16[512,384]{1,0:T(8,128)(2,1)} %collective-permute-done), channel_id=1, source_target_pairs={{0,2},{2,4},{4,6},{6,0},{1,3},{3,5},{5,7},{7,1},{8,10},{10,12},{12... | collective-permute-start | bytes 1179656 | tf_op jit(solution)/shard_map/ppermute | solution.py:26
  132.3 38.4 %copy-start.12 = (bf16[6,512,64]{1,2,0:T(8,128)(2,1)}, bf16[6,512,64]{1,2,0:T(8,128)(2,1)S(1)}, u32[]{:S(2)}) copy-start(bf16[6,512,64]{1,2,0:T(8,128)(2,1)S(1)} %get-tuple-element.109) | copy-start | bytes 1179652
  135.0 83.2 %all-reduce.10.cloned.1.call-start = ((), (), s32[]{:S(2)}) async-start(), calls=%async_computation.4 | async-start | bytes 1572864 | tf_op jit(solution)/shard_map/psum | solution.py:148
  170.2 10.1 %copy-start.26 = (f32[512]{0:T(512)}, f32[512]{0:T(512)S(1)}, u32[]{:S(2)}) copy-start(f32[512]{0:T(512)S(1)} %broadcast_multiply_fusion.5) | copy-start | bytes 6148
  170.7 10.7 %copy-start.48 = (bf16[1536,768]{1,0:T(8,128)(2,1)S(1)}, bf16[1536,768]{1,0:T(8,128)(2,1)}, u32[]{:S(2)}) copy-start(bf16[1536,768]{1,0:T(8,128)(2,1)} %param.35) | copy-start | bytes 7077892
  181.4 36.8 %copy-start.24 = (f32[768]{0:T(1024)S(1)}, f32[768]{0:T(1024)}, u32[]{:S(2)}) copy-start(f32[768]{0:T(1024)} %convert_element_type.185) | copy-start | bytes 9220
  181.4 36.8 %copy-start.27 = (f32[512]{0:T(512)S(1)}, f32[512]{0:T(512)}, u32[]{:S(2)}) copy-start(f32[512]{0:T(512)} %copy-done.26) | copy-start | bytes 6148
  181.4 36.8 %copy-start.30 = (f32[512]{0:T(512)S(1)}, f32[512]{0:T(512)}, u32[]{:S(2)}) copy-start(f32[512]{0:T(512)} %copy-done.29) | copy-start | bytes 6148
  181.4 36.8 %copy-start.39 = (f32[768]{0:T(1024)S(1)}, f32[768]{0:T(1024)}, u32[]{:S(2)}) copy-start(f32[768]{0:T(1024)} %convert_element_type.186) | copy-start | bytes 9220
  183.7 81.3 %all-reduce.12.cloned.1.call-start = ((), (), s32[]{:S(2)}) async-start(), calls=%async_computation.5 | async-start | bytes 1572864 | tf_op jit(solution)/shard_map/psum | solution.py:167
  230.6 38.0 %copy-start.4 = (f32[512,768]{1,0:T(8,128)S(1)}, f32[512,768]{1,0:T(8,128)}, u32[]{:S(2)}) copy-start(f32[512,768]{1,0:T(8,128)} %copy-done.3) | copy-start | bytes 4718596
  230.6 38.0 %copy-start.9 = (bf16[512,768]{1,0:T(8,128)(2,1)S(1)}, bf16[512,768]{1,0:T(8,128)(2,1)}, u32[]{:S(2)}) copy-start(bf16[512,768]{1,0:T(8,128)(2,1)} %all-reduce.8.cloned.1.call-done) | copy-start | bytes 2359300
  230.7 147.6 %reduce-scatter.3.cloned.1.call-start = ((), (), s32[]{:S(2)}) async-start(), calls=%async_computation.6 | async-start | bytes 1966080 | tf_op jit(solution)/shard_map/reduce_scatter | solution.py:196
  342.8 72.0 %reduce-scatter.5.cloned.1.call-start = ((), (), s32[]{:S(2)}) async-start(), calls=%async_computation.7 | async-start | bytes 1966080 | tf_op jit(solution)/shard_map/reduce_scatter | solution.py:199
  343.4 142.0 %all-reduce.14.cloned.1.call-start = ((), (), s32[]{:S(2)}) async-start(), calls=%async_computation.8 | async-start | bytes 1572864 | tf_op jit(solution)/shard_map/psum | solution.py:215
  356.5 58.3 %copy-start.21 = (bf16[768,384]{1,0:T(8,128)(2,1)S(1)}, bf16[768,384]{1,0:T(8,128)(2,1)}, u32[]{:S(2)}) copy-start(bf16[768,384]{1,0:T(8,128)(2,1)} %param.26) | copy-start | bytes 1769476
  418.4 300.7 %all-reduce.16.cloned.1.call-start = ((), (), s32[]{:S(2)}) async-start(), calls=%async_computation.9 | async-start | bytes 28311552 | tf_op jit(solution)/shard_map/psum | solution.py:232
  (43 other events, 130.2 us)
Sparse Core Ops, SparseCore 0:
  10.9 50.6 all-gather.2
  135.1 33.4 all-reduce.7
  183.9 34.3 all-reduce.9
  230.7 34.2 all-reduce.11
  342.9 35.2 reduce-scatter.2
  380.5 34.2 reduce-scatter.4
  418.5 33.2 all-reduce.13
  458.1 260.8 all-reduce.15
